TPU v7x, 256 devices: a whole 4x4x8 slice. The times are simulated.
256 devices in a mesh: east: 32 (over z, y_hi, core), north: 8 (over x, y_lo).
Axes of the slice: x: 4, y: 4 (y_hi: 2, y_lo: 2; y = y_hi * 2 + y_lo), z: 8, core: 2. Of those that a mesh axis runs over, the one named last changes fastest.
Arguments:
- features: bfloat16 [96, 256, 128, 8], P(None, 'east', 'north'), may hold values from -6 to 6
- brick_active: int32 [32, 16, 1], P('east', 'north'), may hold values 0 or 1
- voxel_occupancy: int32 [256, 128, 8], P('east', 'north'), may hold values 0 or 1
- first_weights: bfloat16 [27, 96, 96], replicated, may hold values from -0.125 to 0.125
- second_weights: bfloat16 [27, 96, 96], replicated, may hold values from -0.125 to 0.125
- head: bfloat16 [13, 96], replicated, may hold values from -0.625 to 0.625
- teacher: bfloat16 [13, 256, 128, 8], P(None, 'east', 'north'), may hold values from -6 to 6
Outputs:
- grad_features: bfloat16 [96, 256, 128, 8], P(None, 'east', 'north')
- grad_first: float32 [27, 96, 96], replicated
- grad_second: float32 [27, 96, 96], replicated
All inputs are finite; a program needn't handle non-finite values. No bound on the sum of `brick_active` or of `voxel_occupancy` on one device may be relied on, other than what follows from the above.
Results may differ from a plain program's by a relative error of at most 0.0058.
Values may be sent and summed in bfloat16 or wider, within the bound.
A program may use at most 128 MiB of HBM per device.

v0:
```python
import math
import jax
import jax.numpy as jnp
from jax import lax
from jax.sharding import PartitionSpec as P


def padded(block, sides, width):
    for axis, dim in sides:
        count = lax.axis_size(axis)
        forward = [(i, i + 1) for i in range(count - 1)]
        backward = [(target, source) for source, target in forward]
        low = lax.ppermute(
            lax.slice_in_dim(block, block.shape[dim] - width, None, axis=dim), axis, forward
        )
        high = lax.ppermute(lax.slice_in_dim(block, 0, width, axis=dim), axis, backward)
        block = jnp.concatenate([low, block, high], axis=dim)
    return block


def offset_of(k):
    return (k // 9 - 1, k // 3 % 3 - 1, k % 3 - 1)


def silu_slope(value):
    sig = jax.nn.sigmoid(value)
    return sig * (1.0 + value * (1.0 - sig))


def stacked(field, sign):
    channels, east, north, plane = field.shape
    wider = padded(field, (("east", 1), ("north", 2)), 1)
    flat = wider.reshape(channels, east + 2, (north + 2) * plane)
    flat = jnp.pad(flat, ((0, 0), (0, 0), (1, 1)))
    pieces = []
    for k in range(27):
        de, dn, du = offset_of(k)
        first = 1 + sign * de
        start = (1 + sign * dn) * plane + sign * du + 1
        pieces.append(flat[:, first : first + east, start : start + north * plane])
    return jnp.stack(pieces, 0).reshape(27 * channels, east * north * plane)


def arrange(part, outputs, channels):
    return part.reshape(outputs, 27, channels).transpose(1, 0, 2)


def per_device(
    features, brick_active, voxel_occupancy, first_weights, second_weights, head, teacher
):
    channels = features.shape[0]
    shape = features.shape[1:]
    east, north, upward = shape
    plane = upward + 2
    wide_shape = (channels, east, north, plane)
    flags = jnp.repeat(brick_active, east // brick_active.shape[0], 0)
    flags = jnp.repeat(flags, north // brick_active.shape[1], 1)
    flags = jnp.repeat(flags, upward // brick_active.shape[2], 2)
    mask = jnp.pad((flags * voxel_occupancy).astype(jnp.float32), ((0, 0), (0, 0), (1, 1)))
    flat_mask = mask.reshape(1, -1)
    wide_features = jnp.pad(features, ((0, 0), (0, 0), (0, 0), (1, 1)))
    a0 = jnp.where(mask[None] > 0, wide_features, jnp.zeros_like(wide_features))
    forward_one = first_weights.transpose(1, 0, 2).reshape(channels, 27 * channels)
    forward_two = second_weights.transpose(1, 0, 2).reshape(channels, 27 * channels)
    backward_one = first_weights.transpose(2, 0, 1).reshape(channels, 27 * channels)
    backward_two = second_weights.transpose(2, 0, 1).reshape(channels, 27 * channels)
    stack_zero = stacked(a0, 1)
    p1 = flat_mask * jnp.dot(forward_one, stack_zero, preferred_element_type=jnp.float32)
    a1 = jax.nn.silu(p1).astype(jnp.bfloat16)
    stack_one = stacked(a1.reshape(wide_shape), 1)
    p2 = flat_mask * jnp.dot(forward_two, stack_one, preferred_element_type=jnp.float32)
    a2 = jax.nn.silu(p2).astype(jnp.bfloat16)
    logits = jnp.dot(head, a2, preferred_element_type=jnp.float32)
    wide_teacher = jnp.pad(teacher, ((0, 0), (0, 0), (0, 0), (1, 1))).reshape(teacher.shape[0], -1)
    g_logits = flat_mask * (logits - wide_teacher.astype(jnp.float32))
    g_a2 = jnp.dot(head.astype(jnp.float32).T, g_logits, precision=lax.Precision.HIGHEST)
    g_p2 = (flat_mask * g_a2 * silu_slope(p2)).astype(jnp.bfloat16)
    total_voxels = lax.axis_size("east") * lax.axis_size("north") * east * north * upward
    scale = 1.0 / math.sqrt(total_voxels)
    contract = (((1,), (1,)), ((), ()))
    second_part = lax.dot_general(g_p2, stack_one, contract, preferred_element_type=jnp.float32)
    second_part = arrange(second_part, channels, channels)
    g_a1 = jnp.dot(
        backward_two, stacked(g_p2.reshape(wide_shape), -1), preferred_element_type=jnp.float32
    )
    g_p1 = (flat_mask * g_a1 * silu_slope(p1)).astype(jnp.bfloat16)
    first_part = lax.dot_general(g_p1, stack_zero, contract, preferred_element_type=jnp.float32)
    first_part = arrange(first_part, channels, channels)
    wide_grad = flat_mask * jnp.dot(
        backward_one, stacked(g_p1.reshape(wide_shape), -1), preferred_element_type=jnp.float32
    )
    grad_features = wide_grad.astype(jnp.bfloat16).reshape(wide_shape)[:, :, :, 1 : plane - 1]
    first_part, second_part = lax.psum((first_part, second_part), ("east", "north"))
    return (grad_features, first_part * scale, second_part * scale)


def solution(mesh):
    in_specs = (
        P(None, "east", "north", None),
        P("east", "north", None),
        P("east", "north", None),
        P(),
        P(),
        P(),
        P(None, "east", "north", None),
    )
    out_specs = (P(None, "east", "north", None), P(), P())
    return jax.shard_map(
        per_device, mesh=mesh, in_specs=in_specs, out_specs=out_specs, check_vma=False
    )
```

profile of v0, /device:TPU:8, one launch (start us, length us, event | category | flops | bytes accessed | tf_op | source)
XLA Modules:
  0.0 724.4 jit_solution(11437631143420705263)
XLA Ops:
  11.6 3.0 collective-permute-start
  15.6 4.1 collective-permute-start.3
  19.7 2.7 collective-permute-start.2
  24.3 2.2 copy.105
  26.7 2.2 copy.108
  32.0 2.6 pad_slice_fusion.6
  55.8 14.9 %copy.104 = bf16[27,96,8,160]{3,2,1,0:T(8,128)(2,1)} copy(bf16[27,96,8,160]{1,3,2,0:T(8,128)(2,1)} %constant_dynamic-update-slice_fusion) | data formatting | bytes 13271040 | tf_op jit(solution)/shard_map/stack | solution.py:41
  70.7 17.5 %reshape.185 = bf16[2592,1280]{1,0:T(8,128)(2,1)} reshape(bf16[27,96,8,160]{3,2,1,0:T(8,128)(2,1)} %copy.104) | data formatting | bytes 13271040 | tf_op jit(solution)/shard_map/reshape | solution.py:41
  88.2 5.2 multiply_convert_fusion.1
  96.1 4.9 collective-permute-start.4
  177.5 4.8 collective-permute-start.6
  186.9 2.6 pad_slice_fusion
  210.8 14.9 %copy.107 = bf16[27,96,8,160]{3,2,1,0:T(8,128)(2,1)} copy(bf16[27,96,8,160]{1,3,2,0:T(8,128)(2,1)} %constant_dynamic-update-slice_fusion.30) | data formatting | bytes 13271040 | tf_op jit(solution)/shard_map/stack | solution.py:41
  225.6 17.5 %reshape.189 = bf16[2592,1280]{1,0:T(8,128)(2,1)} reshape(bf16[27,96,8,160]{3,2,1,0:T(8,128)(2,1)} %copy.107) | data formatting | bytes 13271040 | tf_op jit(solution)/shard_map/reshape | solution.py:41
  243.2 4.3 fusion.3
  251.6 5.8 collective-permute-start.8
  331.8 1.9 collective-permute-start.11
  333.7 4.8 collective-permute-start.10
  362.8 14.9 %copy.112 = bf16[27,96,8,160]{3,2,1,0:T(8,128)(2,1)} copy(bf16[27,96,8,160]{1,3,2,0:T(8,128)(2,1)} %constant_dynamic-update-slice_fusion.60) | data formatting | bytes 13271040 | tf_op jit(solution)/shard_map/stack | solution.py:41
  377.6 17.6 %reshape.193 = bf16[2592,1280]{1,0:T(8,128)(2,1)} reshape(bf16[27,96,8,160]{3,2,1,0:T(8,128)(2,1)} %copy.112) | data formatting | bytes 13271040 | tf_op jit(solution)/shard_map/reshape | solution.py:41
  395.3 4.3 fusion.6
  400.0 6.5 collective-permute-start.12
  406.5 6.5 convolution_bitcast_fusion.1
  414.6 4.9 collective-permute-done.13
  419.5 1.9 collective-permute-start.15
  421.4 5.9 collective-permute-start.14
  427.3 6.4 convolution_bitcast_fusion.2
  456.4 14.9 %copy.114 = bf16[27,96,8,160]{3,2,1,0:T(8,128)(2,1)} copy(bf16[27,96,8,160]{1,3,2,0:T(8,128)(2,1)} %constant_dynamic-update-slice_fusion.90) | data formatting | bytes 13271040 | tf_op jit(solution)/shard_map/stack | solution.py:41
  471.3 17.6 %reshape.197 = bf16[2592,1280]{1,0:T(8,128)(2,1)} reshape(bf16[27,96,8,160]{3,2,1,0:T(8,128)(2,1)} %copy.114) | data formatting | bytes 13271040 | tf_op jit(solution)/shard_map/reshape | solution.py:41
  489.0 4.2 fusion.9
  494.4 219.6 %all-reduce.10.cloned.1.call-done = (f32[27,96,96]{2,1,0:T(8,128)}, f32[27,96,96]{2,1,0:T(8,128)}) async-done(((f32[27,96,96]{2,1,0:T(8,128)}, f32[27,96,96]{2,1,0:T(8,128)}), (f32[27,96,96]{2,1,0:T(8,128)}, f32[27,96,96]{2,1,0:T(8,128)})) %all-reduce.10.cloned.1.call-update) | async-done | bytes 1990672 | tf_op jit(solution)/shard_map/psum | solution.py:93
  713.9 3.4 broadcast_multiply_fusion
  (305 shorter events, 265.0 us)
Async XLA Ops:
  7.2 240.3 %copy-start = (bf16[13,96]{1,0:T(8,128)(2,1)S(1)}, bf16[13,96]{1,0:T(8,128)(2,1)}, u32[]{:S(2)}) copy-start(bf16[13,96]{1,0:T(8,128)(2,1)} %param.12) | copy-start | bytes 7492
  7.2 706.8 %all-reduce.10.cloned.1.call-start = ((), (), s32[]{:S(2)}) async-start(), calls=%async_computation | async-start | bytes 5308416 | tf_op jit(solution)/shard_map/psum | solution.py:93
  10.3 5.3 collective-permute-start.1
  11.6 4.0 collective-permute-start
  15.6 13.2 %collective-permute-start.3 = (bf16[96,10,1,10]{0,3,2,1:T(8,128)(2,1)S(1)}, bf16[96,10,1,10]{0,3,2,1:T(8,128)(2,1)S(1)}, u32[]{:S(2)}, u32[]{:S(2)}) collective-permute-start(bf16[96,10,1,10]{0,3,2,1:T(8,128)(2,1)S(1)} %get-tuple-element.12), channel_id=1, source_target_pairs={{1,0},{2,1},{3,2},{4,3},{5,4},{6,5},{7,6},{9,8},{10,9},{11,10},{12... | collective-permute-start | bytes 57608 | tf_op jit(solution)/shard_map/ppermute | solution.py:16
  19.7 9.2 %collective-permute-start.2 = (bf16[96,10,1,10]{0,3,2,1:T(8,128)(2,1)S(1)}, bf16[96,10,1,10]{0,3,2,1:T(8,128)(2,1)S(1)}, u32[]{:S(2)}, u32[]{:S(2)}) collective-permute-start(bf16[96,10,1,10]{0,3,2,1:T(8,128)(2,1)S(1)} %get-tuple-element.11), channel_id=1, source_target_pairs={{0,1},{1,2},{2,3},{3,4},{4,5},{5,6},{6,7},{8,9},{9,10},{10,11},{11... | collective-permute-start | bytes 57608 | tf_op jit(solution)/shard_map/ppermute | solution.py:13
  96.1 78.5 %collective-permute-start.4 = (bf16[96,1,16,10]{0,3,2,1:T(8,128)(2,1)}, bf16[96,1,16,10]{0,3,2,1:T(8,128)(2,1)}, u32[]{:S(2)}, u32[]{:S(2)}) collective-permute-start(bf16[96,1,16,10]{0,3,2,1:T(8,128)(2,1)} %get-tuple-element.18), channel_id=1, source_target_pairs={{0,8},{8,16},{16,24},{24,32},{32,40},{40,48},{48,56},{56,64},{64,7... | collective-permute-start | bytes 92168 | tf_op jit(solution)/shard_map/ppermute | solution.py:13
  100.9 74.6 %collective-permute-start.5 = (bf16[96,1,16,10]{0,3,2,1:T(8,128)(2,1)}, bf16[96,1,16,10]{0,3,2,1:T(8,128)(2,1)S(1)}, u32[]{:S(2)}, u32[]{:S(2)}) collective-permute-start(bf16[96,1,16,10]{0,3,2,1:T(8,128)(2,1)} %get-tuple-element.17), channel_id=1, source_target_pairs={{8,0},{16,8},{24,16},{32,24},{40,32},{48,40},{56,48},{64,56},{72,6... | collective-permute-start | bytes 92168 | tf_op jit(solution)/shard_map/ppermute | solution.py:16
  175.5 7.5 %collective-permute-start.7 = (bf16[96,10,1,10]{0,3,2,1:T(8,128)(2,1)S(1)}, bf16[96,10,1,10]{0,3,2,1:T(8,128)(2,1)S(1)}, u32[]{:S(2)}, u32[]{:S(2)}) collective-permute-start(bf16[96,10,1,10]{0,3,2,1:T(8,128)(2,1)S(1)} %get-tuple-element.10), channel_id=1, source_target_pairs={{1,0},{2,1},{3,2},{4,3},{5,4},{6,5},{7,6},{9,8},{10,9},{11,10},{12... | collective-permute-start | bytes 57608 | tf_op jit(solution)/shard_map/ppermute | solution.py:16
  177.5 6.5 collective-permute-start.6
  243.2 4.3 copy-start.6
  248.3 0.7 copy-start.2
  251.6 79.2 %collective-permute-start.8 = (bf16[96,1,16,10]{0,3,2,1:T(8,128)(2,1)}, bf16[96,1,16,10]{0,3,2,1:T(8,128)(2,1)}, u32[]{:S(2)}, u32[]{:S(2)}) collective-permute-start(bf16[96,1,16,10]{0,3,2,1:T(8,128)(2,1)} %get-tuple-element.16), channel_id=1, source_target_pairs={{0,8},{8,16},{16,24},{24,32},{32,40},{40,48},{48,56},{56,64},{64,7... | collective-permute-start | bytes 92168 | tf_op jit(solution)/shard_map/ppermute | solution.py:13
  257.5 74.3 %collective-permute-start.9 = (bf16[96,1,16,10]{0,3,2,1:T(8,128)(2,1)}, bf16[96,1,16,10]{0,3,2,1:T(8,128)(2,1)S(1)}, u32[]{:S(2)}, u32[]{:S(2)}) collective-permute-start(bf16[96,1,16,10]{0,3,2,1:T(8,128)(2,1)} %get-tuple-element.15), channel_id=1, source_target_pairs={{8,0},{16,8},{24,16},{32,24},{40,32},{48,40},{56,48},{64,56},{72,6... | collective-permute-start | bytes 92168 | tf_op jit(solution)/shard_map/ppermute | solution.py:16
  331.8 7.5 %collective-permute-start.11 = (bf16[96,10,1,10]{0,3,2,1:T(8,128)(2,1)S(1)}, bf16[96,10,1,10]{0,3,2,1:T(8,128)(2,1)S(1)}, u32[]{:S(2)}, u32[]{:S(2)}) collective-permute-start(bf16[96,10,1,10]{0,3,2,1:T(8,128)(2,1)S(1)} %get-tuple-element.8), channel_id=1, source_target_pairs={{1,0},{2,1},{3,2},{4,3},{5,4},{6,5},{7,6},{9,8},{10,9},{11,10},{12... | collective-permute-start | bytes 57608 | tf_op jit(solution)/shard_map/ppermute | solution.py:16
  333.7 6.5 collective-permute-start.10
  377.6 17.6 %copy-start.4 = (bf16[27,96,96]{2,1,0:T(8,128)(2,1)S(1)}, bf16[27,96,96]{2,1,0:T(8,128)(2,1)}, u32[]{:S(2)}) copy-start(bf16[27,96,96]{2,1,0:T(8,128)(2,1)} %param.11) | copy-start | bytes 1492996
  377.6 17.6 %copy-start.7 = (f32[96,1280]{1,0:T(8,128)S(1)}, f32[96,1280]{1,0:T(8,128)}, u32[]{:S(2)}) copy-start(f32[96,1280]{1,0:T(8,128)} %get-tuple-element.76) | copy-start | bytes 1474564
  395.3 11.2 %copy-start.3 = (bf16[96,1280]{1,0:T(8,128)(2,1)S(1)}, bf16[96,1280]{1,0:T(8,128)(2,1)}, u32[]{:S(2)}) copy-start(bf16[96,1280]{1,0:T(8,128)(2,1)} %copy-done.2) | copy-start | bytes 737284
  400.0 14.5 %collective-permute-start.12 = (bf16[96,1,16,10]{0,3,2,1:T(8,128)(2,1)S(1)}, bf16[96,1,16,10]{0,3,2,1:T(8,128)(2,1)S(1)}, u32[]{:S(2)}, u32[]{:S(2)}) collective-permute-start(bf16[96,1,16,10]{0,3,2,1:T(8,128)(2,1)S(1)} %get-tuple-element.14), channel_id=1, source_target_pairs={{0,8},{8,16},{16,24},{24,32},{32,40},{40,48},{48,56},{56,64},{64,7... | collective-permute-start | bytes 92168 | tf_op jit(solution)/shard_map/ppermute | solution.py:13
  413.0 6.5 collective-permute-start.13
  419.5 14.3 %collective-permute-start.15 = (bf16[96,10,1,10]{0,3,2,1:T(8,128)(2,1)S(1)}, bf16[96,10,1,10]{0,3,2,1:T(8,128)(2,1)S(1)}, u32[]{:S(2)}, u32[]{:S(2)}) collective-permute-start(bf16[96,10,1,10]{0,3,2,1:T(8,128)(2,1)S(1)} %get-tuple-element.6), channel_id=1, source_target_pairs={{1,0},{2,1},{3,2},{4,3},{5,4},{6,5},{7,6},{9,8},{10,9},{11,10},{12... | collective-permute-start | bytes 57608 | tf_op jit(solution)/shard_map/ppermute | solution.py:16
  421.4 12.4 %collective-permute-start.14 = (bf16[96,10,1,10]{0,3,2,1:T(8,128)(2,1)S(1)}, bf16[96,10,1,10]{0,3,2,1:T(8,128)(2,1)S(1)}, u32[]{:S(2)}, u32[]{:S(2)}) collective-permute-start(bf16[96,10,1,10]{0,3,2,1:T(8,128)(2,1)S(1)} %get-tuple-element.5), channel_id=1, source_target_pairs={{0,1},{1,2},{2,3},{3,4},{4,5},{5,6},{6,7},{8,9},{9,10},{10,11},{11... | collective-permute-start | bytes 57608 | tf_op jit(solution)/shard_map/ppermute | solution.py:13
  471.3 17.7 %copy-start.5 = (bf16[27,96,96]{2,1,0:T(8,128)(2,1)S(1)}, bf16[27,96,96]{2,1,0:T(8,128)(2,1)}, u32[]{:S(2)}) copy-start(bf16[27,96,96]{2,1,0:T(8,128)(2,1)} %param.10) | copy-start | bytes 1492996
  471.3 246.1 %copy-start.1 = (bf16[13,96]{1,0:T(8,128)(2,1)S(1)}, bf16[13,96]{1,0:T(8,128)(2,1)}, u32[]{:S(2)}) copy-start(bf16[13,96]{1,0:T(8,128)(2,1)} %param.12) | copy-start | bytes 7492
Sparse Core Ops, SparseCore 0:
  433.9 280.0 all-reduce.9
where the time goes:
time: 738 us; the launch traced here: 724 us
  local copies, waits for them, and re-layouts  391 us (53%)
  waiting for transfers between devices  226 us (31%)
  starting transfers between devices  54.3 us (7%)
  matrix products  31.7 us (4%)
  between operations  14.9 us (2%)
    psum x1, waiting for transfers between devices, per_device(): lax.psum((first_part, second_part), ('east', 'north'))  220 us
    unnamed x180, local copies, waits for them, and re-layouts  162 us
    another operation x64, local copies, waits for them, and re-layouts, stacked(): return jnp.stack(pieces, 0).reshape(27 * channels, east * north * plane)  135 us
    reshape x4, local copies, waits for them, and re-layouts, stacked(): return jnp.stack(pieces, 0).reshape(27 * channels, east * north * plane)  70.4 us
    ppermute x8, starting transfers between devices, padded(): lax.ppermute(lax.slice_in_dim(block, block.shape[dim] - width, None, axis...  38.5 us
    ppermute x8, starting transfers between devices, padded(): lax.ppermute(lax.slice_in_dim(block, 0, width, axis=dim), axis, backward)  15.8 us
  transfers between devices with their start and end apart: 17, of which 4 were waited for; matrix products, arithmetic and copies ran while one was open for 31% of the time, Pallas kernels for 0%

commit v1 on v0

--- a/solution.py
+++ b/solution.py
@@ -48,6 +48,12 @@
 def per_device(
     features, brick_active, voxel_occupancy, first_weights, second_weights, head, teacher
 ):
+
+    def detail_cards_here(content, comm_axis, mesh_dim):
+        for w in (comm_axis, mesh_dim):
+            content = lax.psum(content, axis_name=w)
+        return content
+
     channels = features.shape[0]
     shape = features.shape[1:]
     east, north, upward = shape
@@ -90,7 +96,7 @@
         backward_one, stacked(g_p1.reshape(wide_shape), -1), preferred_element_type=jnp.float32
     )
     grad_features = wide_grad.astype(jnp.bfloat16).reshape(wide_shape)[:, :, :, 1 : plane - 1]
-    first_part, second_part = lax.psum((first_part, second_part), ("east", "north"))
+    first_part, second_part = detail_cards_here((first_part, second_part), "east", "north")
     return (grad_features, first_part * scale, second_part * scale)
 
 

time: 738 us -> 882 us (1.20)
  waiting for transfers between devices: 226 us -> 368 us
    psum x1 -> x2, waiting for transfers between devices: 220 us -> 361 us  [detail_cards_here(): content = lax.psum(content, axis_name=w)]
  transfers between devices with their start and end apart: 17 -> 18, of which waited for: 4 -> 5; matrix products, arithmetic and copies ran while one was open for 31% -> 26% of each run, Pallas kernels for 0% -> 0%
where the time goes in v1:
time: 882 us; the launch traced here: 866 us
  local copies, waits for them, and re-layouts  391 us (44%)
  waiting for transfers between devices  368 us (42%)
  starting transfers between devices  54.3 us (6%)
  matrix products  31.6 us (4%)
  between operations  15 us (2%)
    psum x2, waiting for transfers between devices, detail_cards_here(): content = lax.psum(content, axis_name=w)  361 us
    unnamed x180, local copies, waits for them, and re-layouts  162 us
    another operation x64, local copies, waits for them, and re-layouts, stacked(): return jnp.stack(pieces, 0).reshape(27 * channels, east * north * plane)  135 us
    reshape x4, local copies, waits for them, and re-layouts, stacked(): return jnp.stack(pieces, 0).reshape(27 * channels, east * north * plane)  70.3 us
    ppermute x8, starting transfers between devices, padded(): lax.ppermute(lax.slice_in_dim(block, block.shape[dim] - width, None, axis...  38.5 us
  transfers between devices with their start and end apart: 18, of which 5 were waited for; matrix products, arithmetic and copies ran while one was open for 26% of the time, Pallas kernels for 0%

profile of v1, /device:TPU:8, one launch (start us, length us, event | category | flops | bytes accessed | tf_op | source)
XLA Modules:
  0.0 866.0 jit_solution(14470583954235568587)
XLA Ops:
  11.6 3.0 collective-permute-start
  15.6 4.1 collective-permute-start.3
  19.7 2.7 collective-permute-start.2
  24.3 2.2 copy.105
  26.7 2.2 copy.108
  31.9 2.6 pad_slice_fusion.6
  55.8 14.9 %copy.104 = bf16[27,96,8,160]{3,2,1,0:T(8,128)(2,1)} copy(bf16[27,96,8,160]{1,3,2,0:T(8,128)(2,1)} %constant_dynamic-update-slice_fusion) | data formatting | bytes 13271040 | tf_op jit(solution)/shard_map/stack | solution.py:41
  70.7 17.5 %reshape.185 = bf16[2592,1280]{1,0:T(8,128)(2,1)} reshape(bf16[27,96,8,160]{3,2,1,0:T(8,128)(2,1)} %copy.104) | data formatting | bytes 13271040 | tf_op jit(solution)/shard_map/reshape | solution.py:41
  88.3 5.2 multiply_convert_fusion.1
  96.1 4.8 collective-permute-start.4
  175.7 1.9 collective-permute-start.7
  177.6 4.8 collective-permute-start.6
  187.1 2.6 pad_slice_fusion
  211.0 14.9 %copy.107 = bf16[27,96,8,160]{3,2,1,0:T(8,128)(2,1)} copy(bf16[27,96,8,160]{1,3,2,0:T(8,128)(2,1)} %constant_dynamic-update-slice_fusion.30) | data formatting | bytes 13271040 | tf_op jit(solution)/shard_map/stack | solution.py:41
  225.9 17.5 %reshape.189 = bf16[2592,1280]{1,0:T(8,128)(2,1)} reshape(bf16[27,96,8,160]{3,2,1,0:T(8,128)(2,1)} %copy.107) | data formatting | bytes 13271040 | tf_op jit(solution)/shard_map/reshape | solution.py:41
  243.4 4.3 fusion.3
  251.8 5.8 collective-permute-start.8
  334.0 4.8 collective-permute-start.10
  363.1 14.9 %copy.112 = bf16[27,96,8,160]{3,2,1,0:T(8,128)(2,1)} copy(bf16[27,96,8,160]{1,3,2,0:T(8,128)(2,1)} %constant_dynamic-update-slice_fusion.60) | data formatting | bytes 13271040 | tf_op jit(solution)/shard_map/stack | solution.py:41
  378.0 17.6 %reshape.193 = bf16[2592,1280]{1,0:T(8,128)(2,1)} reshape(bf16[27,96,8,160]{3,2,1,0:T(8,128)(2,1)} %copy.112) | data formatting | bytes 13271040 | tf_op jit(solution)/shard_map/reshape | solution.py:41
  395.6 4.3 fusion.6
  400.3 6.5 collective-permute-start.12
  406.8 6.5 convolution_bitcast_fusion.1
  414.9 4.9 collective-permute-done.13
  421.7 5.9 collective-permute-start.14
  427.6 6.4 convolution_bitcast_fusion.2
  451.1 272.8 %all-reduce.12.cloned.1.call-done = (f32[27,96,96]{2,1,0:T(8,128)}, f32[27,96,96]{2,1,0:T(8,128)}) async-done(((f32[27,96,96]{2,1,0:T(8,128)}, f32[27,96,96]{2,1,0:T(8,128)}), (f32[27,96,96]{2,1,0:T(8,128)}, f32[27,96,96]{2,1,0:T(8,128)})) %all-reduce.12.cloned.1.call-update) | async-done | bytes 1990672 | tf_op jit(solution)/shard_map/psum | solution.py:54
  729.6 14.9 %copy.114 = bf16[27,96,8,160]{3,2,1,0:T(8,128)(2,1)} copy(bf16[27,96,8,160]{1,3,2,0:T(8,128)(2,1)} %constant_dynamic-update-slice_fusion.90) | data formatting | bytes 13271040 | tf_op jit(solution)/shard_map/stack | solution.py:41
  744.5 17.6 %reshape.197 = bf16[2592,1280]{1,0:T(8,128)(2,1)} reshape(bf16[27,96,8,160]{3,2,1,0:T(8,128)(2,1)} %copy.114) | data formatting | bytes 13271040 | tf_op jit(solution)/shard_map/reshape | solution.py:41
  762.1 4.2 fusion.9
  767.5 88.0 %all-reduce.14.cloned.1.call-done = (f32[27,96,96]{2,1,0:T(8,128)}, f32[27,96,96]{2,1,0:T(8,128)}) async-done(((f32[27,96,96]{2,1,0:T(8,128)}, f32[27,96,96]{2,1,0:T(8,128)}), (f32[27,96,96]{2,1,0:T(8,128)}, f32[27,96,96]{2,1,0:T(8,128)})) %all-reduce.14.cloned.1.call-update) | async-done | bytes 1990672 | tf_op jit(solution)/shard_map/psum | solution.py:54
  855.5 3.4 broadcast_multiply_fusion
  (308 shorter events, 267.3 us)
Async XLA Ops:
  7.2 240.5 %copy-start = (bf16[13,96]{1,0:T(8,128)(2,1)S(1)}, bf16[13,96]{1,0:T(8,128)(2,1)}, u32[]{:S(2)}) copy-start(bf16[13,96]{1,0:T(8,128)(2,1)} %param.12) | copy-start | bytes 7492
  7.2 716.7 %all-reduce.12.cloned.1.call-start = ((), (), s32[]{:S(2)}) async-start(), calls=%async_computation | async-start | bytes 5308416 | tf_op jit(solution)/shard_map/psum | solution.py:54
  10.3 5.3 collective-permute-start.1
  11.6 4.0 collective-permute-start
  15.6 13.2 %collective-permute-start.3 = (bf16[96,10,1,10]{0,3,2,1:T(8,128)(2,1)S(1)}, bf16[96,10,1,10]{0,3,2,1:T(8,128)(2,1)S(1)}, u32[]{:S(2)}, u32[]{:S(2)}) collective-permute-start(bf16[96,10,1,10]{0,3,2,1:T(8,128)(2,1)S(1)} %get-tuple-element.14), channel_id=1, source_target_pairs={{1,0},{2,1},{3,2},{4,3},{5,4},{6,5},{7,6},{9,8},{10,9},{11,10},{12... | collective-permute-start | bytes 57608 | tf_op jit(solution)/shard_map/ppermute | solution.py:16
  19.7 9.2 %collective-permute-start.2 = (bf16[96,10,1,10]{0,3,2,1:T(8,128)(2,1)S(1)}, bf16[96,10,1,10]{0,3,2,1:T(8,128)(2,1)S(1)}, u32[]{:S(2)}, u32[]{:S(2)}) collective-permute-start(bf16[96,10,1,10]{0,3,2,1:T(8,128)(2,1)S(1)} %get-tuple-element.13), channel_id=1, source_target_pairs={{0,1},{1,2},{2,3},{3,4},{4,5},{5,6},{6,7},{8,9},{9,10},{10,11},{11... | collective-permute-start | bytes 57608 | tf_op jit(solution)/shard_map/ppermute | solution.py:13
  96.1 78.6 %collective-permute-start.4 = (bf16[96,1,16,10]{0,3,2,1:T(8,128)(2,1)}, bf16[96,1,16,10]{0,3,2,1:T(8,128)(2,1)}, u32[]{:S(2)}, u32[]{:S(2)}) collective-permute-start(bf16[96,1,16,10]{0,3,2,1:T(8,128)(2,1)} %get-tuple-element.20), channel_id=1, source_target_pairs={{0,8},{8,16},{16,24},{24,32},{32,40},{40,48},{48,56},{56,64},{64,7... | collective-permute-start | bytes 92168 | tf_op jit(solution)/shard_map/ppermute | solution.py:13
  100.9 74.7 %collective-permute-start.5 = (bf16[96,1,16,10]{0,3,2,1:T(8,128)(2,1)}, bf16[96,1,16,10]{0,3,2,1:T(8,128)(2,1)S(1)}, u32[]{:S(2)}, u32[]{:S(2)}) collective-permute-start(bf16[96,1,16,10]{0,3,2,1:T(8,128)(2,1)} %get-tuple-element.19), channel_id=1, source_target_pairs={{8,0},{16,8},{24,16},{32,24},{40,32},{48,40},{56,48},{64,56},{72,6... | collective-permute-start | bytes 92168 | tf_op jit(solution)/shard_map/ppermute | solution.py:16
  175.7 7.5 collective-permute-start.7
  177.6 6.5 collective-permute-start.6
  243.4 4.3 copy-start.6
  248.5 0.7 copy-start.2
  251.8 79.2 %collective-permute-start.8 = (bf16[96,1,16,10]{0,3,2,1:T(8,128)(2,1)}, bf16[96,1,16,10]{0,3,2,1:T(8,128)(2,1)}, u32[]{:S(2)}, u32[]{:S(2)}) collective-permute-start(bf16[96,1,16,10]{0,3,2,1:T(8,128)(2,1)} %get-tuple-element.18), channel_id=1, source_target_pairs={{0,8},{8,16},{16,24},{24,32},{32,40},{40,48},{48,56},{56,64},{64,7... | collective-permute-start | bytes 92168 | tf_op jit(solution)/shard_map/ppermute | solution.py:13
  257.7 74.3 %collective-permute-start.9 = (bf16[96,1,16,10]{0,3,2,1:T(8,128)(2,1)}, bf16[96,1,16,10]{0,3,2,1:T(8,128)(2,1)S(1)}, u32[]{:S(2)}, u32[]{:S(2)}) collective-permute-start(bf16[96,1,16,10]{0,3,2,1:T(8,128)(2,1)} %get-tuple-element.17), channel_id=1, source_target_pairs={{8,0},{16,8},{24,16},{32,24},{40,32},{48,40},{56,48},{64,56},{72,6... | collective-permute-start | bytes 92168 | tf_op jit(solution)/shard_map/ppermute | solution.py:16
  332.1 7.5 collective-permute-start.11
  334.0 6.5 collective-permute-start.10
  378.0 17.6 %copy-start.4 = (bf16[27,96,96]{2,1,0:T(8,128)(2,1)S(1)}, bf16[27,96,96]{2,1,0:T(8,128)(2,1)}, u32[]{:S(2)}) copy-start(bf16[27,96,96]{2,1,0:T(8,128)(2,1)} %param.11) | copy-start | bytes 1492996
  378.0 17.6 %copy-start.7 = (f32[96,1280]{1,0:T(8,128)S(1)}, f32[96,1280]{1,0:T(8,128)}, u32[]{:S(2)}) copy-start(f32[96,1280]{1,0:T(8,128)} %get-tuple-element.78) | copy-start | bytes 1474564
  395.6 11.2 %copy-start.3 = (bf16[96,1280]{1,0:T(8,128)(2,1)S(1)}, bf16[96,1280]{1,0:T(8,128)(2,1)}, u32[]{:S(2)}) copy-start(bf16[96,1280]{1,0:T(8,128)(2,1)} %copy-done.2) | copy-start | bytes 737284
  400.3 14.5 %collective-permute-start.12 = (bf16[96,1,16,10]{0,3,2,1:T(8,128)(2,1)S(1)}, bf16[96,1,16,10]{0,3,2,1:T(8,128)(2,1)S(1)}, u32[]{:S(2)}, u32[]{:S(2)}) collective-permute-start(bf16[96,1,16,10]{0,3,2,1:T(8,128)(2,1)S(1)} %get-tuple-element.16), channel_id=1, source_target_pairs={{0,8},{8,16},{16,24},{24,32},{32,40},{40,48},{48,56},{56,64},{64,7... | collective-permute-start | bytes 92168 | tf_op jit(solution)/shard_map/ppermute | solution.py:13
  413.3 6.5 collective-permute-start.13
  419.8 14.4 %collective-permute-start.15 = (bf16[96,10,1,10]{0,3,2,1:T(8,128)(2,1)S(1)}, bf16[96,10,1,10]{0,3,2,1:T(8,128)(2,1)S(1)}, u32[]{:S(2)}, u32[]{:S(2)}) collective-permute-start(bf16[96,10,1,10]{0,3,2,1:T(8,128)(2,1)S(1)} %get-tuple-element.8), channel_id=1, source_target_pairs={{1,0},{2,1},{3,2},{4,3},{5,4},{6,5},{7,6},{9,8},{10,9},{11,10},{12... | collective-permute-start | bytes 57608 | tf_op jit(solution)/shard_map/ppermute | solution.py:16
  421.7 12.4 %collective-permute-start.14 = (bf16[96,10,1,10]{0,3,2,1:T(8,128)(2,1)S(1)}, bf16[96,10,1,10]{0,3,2,1:T(8,128)(2,1)S(1)}, u32[]{:S(2)}, u32[]{:S(2)}) collective-permute-start(bf16[96,10,1,10]{0,3,2,1:T(8,128)(2,1)S(1)} %get-tuple-element.7), channel_id=1, source_target_pairs={{0,1},{1,2},{2,3},{3,4},{4,5},{5,6},{6,7},{8,9},{9,10},{10,11},{11... | collective-permute-start | bytes 57608 | tf_op jit(solution)/shard_map/ppermute | solution.py:13
  434.1 421.4 %all-reduce.14.cloned.1.call-start = ((), (), s32[]{:S(2)}) async-start(), calls=%async_computation.1 | async-start | bytes 5308416 | tf_op jit(solution)/shard_map/psum | solution.py:54
  744.5 17.6 %copy-start.5 = (bf16[27,96,96]{2,1,0:T(8,128)(2,1)S(1)}, bf16[27,96,96]{2,1,0:T(8,128)(2,1)}, u32[]{:S(2)}) copy-start(bf16[27,96,96]{2,1,0:T(8,128)(2,1)} %param.10) | copy-start | bytes 1492996
  744.5 114.4 %copy-start.1 = (bf16[13,96]{1,0:T(8,128)(2,1)S(1)}, bf16[13,96]{1,0:T(8,128)(2,1)}, u32[]{:S(2)}) copy-start(bf16[13,96]{1,0:T(8,128)(2,1)} %param.12) | copy-start | bytes 7492
Sparse Core Ops, SparseCore 0:
  434.2 289.5 all-reduce.11
  726.6 128.8 all-reduce.13
